TPU v7x, 1024 devices: a whole 4x8x16 slice. The times are simulated.
1024 devices in a mesh: ctx: 128 (over y, z), tp: 8 (over x, core).
Axes of the slice: x: 4, y: 8, z: 16, core: 2. Of those that a mesh axis runs over, the one named last changes fastest.
Arguments:
- query: bfloat16 [32768, 8192], P('ctx', 'tp'), may hold values from -6 to 6
- gated: bfloat16 [32768, 8192], P('ctx', 'tp'), may hold values from -6 to 6
- cotangent: bfloat16 [32768, 8192], P('ctx', 'tp'), may hold values from -6 to 6
- rate: float32 [8192, 8], P('tp'), may hold values from 1e-08 to 0.03
- residue: float32 [8192, 8], P('tp'), may hold values from -2 to 2
- gain: float32 [8192], P('tp'), may hold values from 0.5 to 1.5
Outputs:
- normed: bfloat16 [32768, 8192], P('ctx', 'tp')
- query_grad: bfloat16 [32768, 8192], P('ctx', 'tp')
- gated_grad: bfloat16 [32768, 8192], P('ctx', 'tp')
All inputs are finite; a program needn't handle non-finite values.
Results may differ from a plain program's by a relative error of at most 0.0015.
Values sent between devices are 32-bit elements; how exact they have to be, the bound alone decides.
A program may use at most 64 MiB of HBM per device.

v0:
```python
import jax
import jax.numpy as jnp
from jax import lax
from jax.sharding import PartitionSpec as P


def entering(part, axis, combine, identity, reverse):
    count = lax.axis_size(axis)
    place = lax.axis_index(axis)
    ahead = count - 1 - place if reverse else place
    gathered = jax.tree.map(lambda a: lax.all_gather(a, axis), part)
    state = jax.tree.map(lambda a, e: jnp.zeros_like(a) + jnp.asarray(e, a.dtype), part, identity)

    def one(lap, state):
        source = count - 1 - lap if reverse else lap
        return combine(
            state, jax.tree.map(lambda a: lax.dynamic_index_in_dim(a, source, 0, False), gathered)
        )

    return lax.fori_loop(0, ahead, one, state)


def per_device(query, gated, cotangent, rate, residue, gain):
    tokens, width = query.shape
    seq_total = tokens * lax.axis_size("ctx")
    total_width = width * lax.axis_size("tp")
    blk = 16
    nblocks = tokens // blk
    rate_t = jnp.transpose(rate)
    weight_t = jnp.transpose(residue * jnp.sqrt(2.0 * rate + 1.0 / seq_total))
    pos = jnp.arange(blk).astype(jnp.float32)
    lam_pow = jnp.exp(-rate_t[None] * pos[:, None, None])
    hvals = jnp.sum(lam_pow * weight_t[None], axis=1)
    step_decay = jnp.exp(-rate_t * blk)
    into = jnp.exp(-rate_t[None] * (pos[:, None, None] + 1.0)) * weight_t[None]
    back_tab = jnp.exp(-rate_t[None] * (blk - pos)[:, None, None]) * weight_t[None]
    block_pos = jnp.arange(nblocks).astype(jnp.float32)
    lead_pow = jnp.exp(-rate_t[None] * (blk * block_pos)[:, None, None])
    tail_pow = lead_pow[::-1]
    zeros_state = jnp.zeros_like(rate_t)
    one_count = jnp.ones((), jnp.float32)
    zero_count = jnp.zeros((), jnp.float32)

    def combine(earlier, later):
        factor = jnp.exp(-rate_t * tokens * later[0])
        return (earlier[0] + later[0], factor * earlier[1] + later[1])

    ublocks = gated.astype(jnp.float32).reshape(nblocks, blk, width)
    intra = hvals[0][None, None] * ublocks
    for lag in range(1, blk):
        moved = jnp.pad(ublocks[:, : blk - lag], ((0, 0), (lag, 0), (0, 0)))
        intra = intra + hvals[lag][None, None] * moved
    ends = jnp.sum(ublocks[:, :, None, :] * lam_pow[::-1][None], axis=1)

    def fchain(state, end_blk):
        return (step_decay * state + end_blk, state)

    final, starts = lax.scan(fchain, zeros_state, ends)
    incoming = entering((one_count, final), "ctx", combine, (zero_count, zeros_state), False)[1]
    starts = starts + lead_pow * incoming[None]
    conv = intra + jnp.sum(starts[:, None] * into[None], axis=2)
    conv = conv.reshape(tokens, width)
    qf = query.astype(jnp.float32)
    mixed = qf * conv
    scaled = gain[None] * cotangent.astype(jnp.float32)
    square_sum, cross_sum = lax.psum(
        (jnp.sum(mixed * mixed, axis=1), jnp.sum(scaled * mixed, axis=1)), "tp"
    )
    inv_rms = (1.0 / jnp.sqrt(square_sum / total_width + 1e-06))[:, None]
    proj = (cross_sum / total_width)[:, None]
    normed = (mixed * inv_rms * gain[None]).astype(jnp.bfloat16)
    mixed_grad = inv_rms * scaled - mixed * inv_rms**3 * proj
    query_grad = (mixed_grad * conv).astype(jnp.bfloat16)
    grad_blocks = (mixed_grad * qf).reshape(nblocks, blk, width)
    intra_back = hvals[0][None, None] * grad_blocks
    for lag in range(1, blk):
        moved = jnp.pad(grad_blocks[:, lag:], ((0, 0), (0, lag), (0, 0)))
        intra_back = intra_back + hvals[lag][None, None] * moved
    begins = jnp.sum(grad_blocks[:, :, None, :] * lam_pow[None], axis=1)

    def bchain(state, begin_blk):
        return (step_decay * state + begin_blk, state)

    first, later = lax.scan(bchain, zeros_state, begins, reverse=True)
    behind = entering((one_count, first), "ctx", combine, (zero_count, zeros_state), True)[1]
    later = later + tail_pow * behind[None]
    gated_grad = intra_back + jnp.sum(later[:, None] * back_tab[None], axis=2)
    return (normed, query_grad, gated_grad.reshape(tokens, width).astype(jnp.bfloat16))


def solution(mesh):
    in_specs = (
        P("ctx", "tp"),
        P("ctx", "tp"),
        P("ctx", "tp"),
        P("tp", None),
        P("tp", None),
        P("tp"),
    )
    out_specs = (P("ctx", "tp"), P("ctx", "tp"), P("ctx", "tp"))
    return jax.shard_map(
        per_device, mesh=mesh, in_specs=in_specs, out_specs=out_specs, check_vma=False
    )
```

profile of v0, /device:TPU:6, one launch (start us, length us, event | category | flops | bytes accessed | tf_op | source)
XLA Modules:
  0.0 1177.6 jit_solution(16864045550551921812)
XLA Ops:
  17.0 1.4 dynamic-slice
  19.1 295.1 %all-reduce.30 = f32[128]{0:T(128)} all-reduce(f32[128]{0:T(128)S(1)} %dynamic-update-slice), channel_id=1, replica_groups=mesh['ctx'=128,'tp'=8] {'ctx'}, use_global_device_ids=true, to_apply=%add.30 | all-reduce | flops 128 | bytes 1024
  315.6 1.6 multiply_exponential_fusion
  317.2 2.9 multiply_reduce_fusion.2
  320.4 3.7 add_add_fusion
  324.4 10.0 all-reduce.31
  334.4 2.7 convert_multiply_fusion
  350.5 465.7 %all-gather.7.cloned.1.call-done = f32[1024,1024]{1,0:T(8,128)} async-done(((f32[8,1024]{1,0:T(8,128)}), f32[1024,1024]{1,0:T(8,128)}) %all-gather.7.cloned.1.call-update) | async-done | bytes 4194320 | tf_op jit(solution)/shard_map/all_gather | solution.py:11
  816.2 344.9 %while.59 = (s32[]{:T(128)}, f32[8,1024]{1,0:T(8,128)S(1)}, s32[]{:T(128)}, f32[128]{0:T(128)}, f32[8,1024]{1,0:T(8,128)S(1)}, /*index=5*/f32[128,8,1024]{2,1,0:...) while((s32[]{:T(128)}, f32[8,1024]{1,0:T(8,128)S(1)}, s32[]{:T(128)}, ...), condition=%wide.region_15.16_spmd, body=%wide.region_14.15_spmd.sunk | while | flops 24583 | bytes 131267 | solution.py:20
  821.7 1.3 dynamic_slice.58
  827.1 1.3 dynamic_slice.58
  832.5 1.3 dynamic_slice.58
  838.0 1.3 dynamic_slice.58
  840.7 1.3 dynamic_slice.58
  843.4 1.3 dynamic_slice.58
  846.1 1.3 dynamic_slice.58
  848.8 1.3 dynamic_slice.58
  851.5 1.3 dynamic_slice.58
  854.2 1.3 dynamic_slice.58
  857.0 1.3 dynamic_slice.58
  859.7 1.3 dynamic_slice.58
  862.4 1.3 dynamic_slice.58
  865.1 1.3 dynamic_slice.58
  867.8 1.3 dynamic_slice.58
  873.2 1.3 dynamic_slice.58
  878.7 1.3 dynamic_slice.58
  884.1 1.3 dynamic_slice.58
  889.5 1.3 dynamic_slice.58
  892.2 1.3 dynamic_slice.58
  894.9 1.3 dynamic_slice.58
  897.7 1.3 dynamic_slice.58
  900.4 1.3 dynamic_slice.58
  903.1 1.3 dynamic_slice.58
  905.8 1.3 dynamic_slice.58
  908.5 1.3 dynamic_slice.58
  911.2 1.3 dynamic_slice.58
  913.9 1.3 dynamic_slice.58
  916.7 1.3 dynamic_slice.58
  919.4 1.3 dynamic_slice.58
  924.8 1.3 dynamic_slice.58
  930.2 1.3 dynamic_slice.58
  935.7 1.3 dynamic_slice.58
  941.1 1.3 dynamic_slice.58
  943.8 1.3 dynamic_slice.58
  946.5 1.3 dynamic_slice.58
  1161.1 1.4 multiply_add_fusion
  1162.6 4.0 multiply_reduce_fusion
  1166.6 4.1 add_convert_fusion
  (377 shorter events, 242.1 us)
Async XLA Ops:
  7.2 308.4 %all-gather.5.cloned.1.call-start = ((), (), s32[]{:S(2)}) async-start(), calls=%async_computation | async-start | bytes 4227072 | tf_op jit(solution)/shard_map/all_gather | solution.py:11
  12.8 0.6 copy-start.4
  13.4 802.8 %all-gather.7.cloned.1.call-start = ((), (), s32[]{:S(2)}) async-start(), calls=%async_computation.1 | async-start | bytes 4227072 | tf_op jit(solution)/shard_map/all_gather | solution.py:11
  315.4 4.8 copy-start.8
  315.4 4.8 copy-start.9
  315.4 4.8 copy-start.10
  315.4 4.8 copy-start.11
  315.5 4.8 copy-start.12
  315.5 4.8 copy-start.13
  315.5 4.8 copy-start.14
  315.5 4.8 copy-start.15
  315.5 4.8 copy-start.16
  315.5 4.8 copy-start.17
  315.5 4.8 copy-start.18
  315.5 4.8 copy-start.19
  320.3 3.7 copy-start.5
  320.3 3.7 copy-start.6
  320.3 3.7 copy-start.20
  338.9 0.6 copy-start.3
  338.9 5.6 copy-start.7
  1161.1 5.5 copy-start
  1161.1 5.5 copy-start.1
  1161.1 5.5 copy-start.2
Sparse Core Ops, SparseCore 0:
  13.5 158.2 all-gather.4
  339.6 476.5 all-gather.6
where the time goes:
time: 1190 us; the launch traced here: 1180 us
  waiting for transfers between devices  466 us (39%)
  blocking collectives  305 us (26%)
  local copies, waits for them, and re-layouts  182 us (15%)
  other arithmetic  126 us (11%)
  loops' own time  83.7 us (7%)
  between operations  14.6 us (1%)
    all_gather x2, waiting for transfers between devices, entering(): gathered = jax.tree.map(lambda a: lax.all_gather(a, axis), part)  466 us
    unnamed x1, blocking collectives  295 us
    dynamic_slice x127, local copies, waits for them, and re-layouts, one(): lax.dynamic_index_in_dim(a, source, 0, False)  163 us
    add x127, other arithmetic, combine(): return (earlier[0] + later[0], factor * earlier[1] + later[1])  98.9 us
    another operation x2, loops' own time, entering(): return lax.fori_loop(0, ahead, one, state)  82.7 us
  transfers between devices with their start and end apart: 2, of which 1 were waited for; matrix products, arithmetic and copies ran while one was open for 2% of the time, Pallas kernels for 0%

commit v1 on v0

v1 whole, which is shorter than its diff:
```python
import functools

import jax
import jax.numpy as jnp
from jax import lax
from jax.experimental import pallas as pl
from jax.experimental.pallas import tpu as pltpu
from jax.sharding import PartitionSpec as P

MESH = pl.DeviceIdType.MESH
NJ = 4
MODES = 8
SUB = 8
LANES = 128
F32 = jnp.float32


def kernel(
    ny, nk, ntp,
    query, gated, cotangent, rate, residue, gain,
    normed, query_grad, gated_grad,
    qb, gb, cb, rate_v, residue_v, gain_v,
    u, y, qf, sf, cg, nm, qg,
    rt, lam_t, w_t, cf_t, cb_t, ex_t,
    states, incoming, z1_buf, z2_buf, y_buf, g_out, t_out, in_out,
    sq, cs, msg, tp_buf, inv_t, proj_t,
    in_sem, out_sem, send_sem, recv_sem, tp_send, tp_recv,
):
    tokens, width = qb.shape
    groups = width // LANES
    part = groups // NJ
    steps = tokens // SUB
    seq_total = tokens * NJ * nk * ny
    total_width = width * ntp
    place = lax.axis_index("ctx")
    column = lax.axis_index("tp")
    yy = place // (NJ * nk)
    kk = lax.rem(place // NJ, nk)
    jj = lax.rem(place, NJ)

    def at(y_, k_, j_):
        return (y_ * nk + k_) * NJ + j_

    near = [at(yy, kk, lax.rem(jj + i, NJ)) for i in range(1, NJ)]
    across = [at(yy, lax.rem(kk + i, nk), jj) for i in range(1, nk)]
    rows = [at(lax.rem(yy + i, ny), kk, jj) for i in range(1, ny)]
    mates = [lax.rem(column + i, ntp) for i in range(1, ntp)]

    barrier = pltpu.get_barrier_semaphore()
    for other in near + across + rows:
        pl.semaphore_signal(barrier, inc=1, device_id=(other, column), device_id_type=MESH)
    for mate in mates:
        pl.semaphore_signal(barrier, inc=1, device_id=(place, mate), device_id_type=MESH)

    loads = [
        pltpu.make_async_copy(src, dst, in_sem.at[n])
        for n, (src, dst) in enumerate(
            [(rate, rate_v), (residue, residue_v), (gated, gb), (query, qb), (cotangent, cb), (gain, gain_v)]
        )
    ]
    for load in loads:
        load.start()

    seg = lax.broadcasted_iota(jnp.int32, (SUB, LANES), 0)
    segf = seg.astype(F32)
    lane = lax.broadcasted_iota(jnp.int32, (SUB, LANES), 1)

    def cols(c):
        return pl.ds(pl.multiple_of(c * LANES, LANES), LANES)

    def wide(row):
        return jnp.broadcast_to(row, (SUB, LANES))

    def token_rows(j):
        return pl.ds(j, SUB, stride=steps)

    def spread(src, dst, scale=None):
        @pl.loop(0, groups)
        def _(c):
            for t in range(0, tokens, 32):
                tile = src[t : t + 32, cols(c)].astype(F32)
                dst[c, t : t + 32, :] = tile if scale is None else tile * scale[pl.ds(c, 1), :]

    def gather_segments(c, state, reverse):
        for m in range(MODES):
            r = wide(rate_v[pl.ds(m, 1), cols(c)])
            x = state[m]
            for hop in (1, 2, 4):
                decay = jnp.exp(-r * float(steps * hop))
                if reverse:
                    x = x + jnp.where(seg < SUB - hop, decay, 0.0) * pltpu.roll(x, SUB - hop, 0)
                else:
                    x = x + jnp.where(seg >= hop, decay, 0.0) * pltpu.roll(x, hop, 0)
            if reverse:
                states[1, c, pl.ds(m, 1), :] = x[0:1]
                ex_t[c, m] = jnp.where(seg < SUB - 1, pltpu.roll(x, SUB - 1, 0), 0.0)
            else:
                states[0, c, pl.ds(m, 1), :] = x[SUB - 1 : SUB]
                ex_t[c, m] = jnp.where(seg >= 1, pltpu.roll(x, 1, 0), 0.0)

    def add_up(terms):
        while len(terms) > 1:
            terms = [a + b for a, b in zip(terms[::2], terms[1::2])] + ([terms[-1]] if len(terms) % 2 else [])
        return terms[0]

    loads[0].wait()
    loads[1].wait()

    @pl.loop(0, groups)
    def _(c):
        rates = rate_v[:, cols(c)]
        rt[c] = rates
        residue_v[:, cols(c)] = residue_v[:, cols(c)] * jnp.sqrt(2.0 * rates + 1.0 / seq_total)
        for m in range(MODES):
            lam_t[c, m] = jnp.exp(-wide(rate_v[pl.ds(m, 1), cols(c)]))

    loads[2].wait()
    spread(gb, u)

    @pl.loop(0, groups)
    def _(c):
        lam = [lam_t[c, m] for m in range(MODES)]

        def block(jb, state):
            for inner in range(4):
                value = u[c, token_rows(jb * 4 + inner), :]
                state = [lam[m] * state[m] + value for m in range(MODES)]
            return state

        state = lax.fori_loop(0, steps // 4, block, [jnp.zeros((SUB, LANES), F32)] * MODES)
        gather_segments(c, state, False)

    pl.semaphore_wait(barrier, len(near) + len(across) + len(rows) + len(mates))

    sends = []

    def copy(src, dst, way, number, device):
        out = pltpu.make_async_remote_copy(
            src_ref=src,
            dst_ref=dst,
            send_sem=send_sem.at[way, number],
            recv_sem=recv_sem.at[way, number],
            device_id=device,
            device_id_type=MESH,
        )
        sends.append(out)
        return out

    def exchange(way):
        mirror = lambda p, n: (n - 1 - p) if way else p
        slot = lambda p, i, n: lax.rem(p + n - i, n)
        j_me, k_me, y_me = mirror(jj, NJ), mirror(kk, nk), mirror(yy, ny)
        j_src = [mirror(slot(jj, i, NJ), NJ) for i in range(NJ)]
        k_src = [mirror(slot(kk, i, nk), nk) for i in range(nk)]
        y_src = [mirror(slot(yy, i, ny), ny) for i in range(ny)]
        quarter = pl.ds(jj * part, part)

        def decay(blocks):
            count = (blocks * tokens).astype(F32) if hasattr(blocks, "astype") else float(blocks * tokens)
            return jnp.exp(-rt[quarter] * count)

        def before(source, here, blocks_apart):
            gap = jnp.maximum(here - source - 1, 0)
            return jnp.where(source < here, decay(gap * blocks_apart), 0.0)

        first = [
            copy(
                states.at[way, pl.ds(lax.rem(jj + i, NJ) * part, part)],
                z1_buf.at[way, i - 1], way, i - 1, (near[i - 1], column),
            )
            for i in range(1, NJ)
        ]
        for one in first:
            one.start()
        yield
        weights = [decay(NJ - 1 - j_src[i]) for i in range(NJ)]
        own = states[way, quarter]
        for one in first:
            one.wait_recv()
        members = [own] + [z1_buf[way, i] for i in range(NJ - 1)]
        total = add_up([a * b for a, b in zip(weights, members)])
        g_out[way] = total
        base = NJ - 1
        second = [
            copy(g_out.at[way], z2_buf.at[way, i - 1], way, base + i - 1, (across[i - 1], column))
            for i in range(1, nk)
        ]
        for one in second:
            one.start()
        yield
        within = []
        for i in range(NJ):
            target = mirror(lax.rem(jj + i, NJ), NJ)
            within.append((target, add_up([before(j_src[s], target, 1) * members[s] for s in range(NJ)])))
        weights = [decay(NJ * (nk - 1 - k_src[i])) for i in range(nk)]
        ahead = [before(k_src[i], k_me, NJ) for i in range(nk)]
        for one in second:
            one.wait_recv()
        totals = [total] + [z2_buf[way, i] for i in range(nk - 1)]
        row = add_up([a * b for a, b in zip(weights, totals)])
        t_out[way] = row
        base = base + nk - 1
        third = [
            copy(t_out.at[way], y_buf.at[way, i - 1], way, base + i - 1, (rows[i - 1], column))
            for i in range(1, ny)
        ]
        for one in third:
            one.start()
        yield
        in_row = add_up([a * b for a, b in zip(ahead, totals)])
        weights = [before(y_src[i], y_me, NJ * nk) for i in range(ny)]
        to_group = decay(NJ * k_me)
        reach = [decay(target) for target, _ in within]
        for one in third:
            one.wait_recv()
        rows_in = [row] + [y_buf[way, i] for i in range(ny - 1)]
        enters = in_row + to_group * add_up([a * b for a, b in zip(weights, rows_in)])
        base = base + ny - 1
        fourth = []
        for i in range(NJ):
            result = within[i][1] + reach[i] * enters
            if i == 0:
                incoming[way, quarter] = result
            else:
                in_out[way, i - 1] = result
                one = copy(
                    in_out.at[way, i - 1], incoming.at[way, quarter],
                    way, base + i - 1, (near[i - 1], column),
                )
                one.start()
                fourth.append(one)
        yield
        for one in fourth:
            one.wait_recv()
        yield

    forward = exchange(0)
    next(forward)

    @pl.loop(0, groups)
    def _(c):
        for m in range(MODES):
            w = wide(residue_v[pl.ds(m, 1), cols(c)])
            r = wide(rate_v[pl.ds(m, 1), cols(c)])
            w_t[c, m] = w
            cf_t[c, m] = w * jnp.exp(-r * (segf * float(steps) + 1.0))
            cb_t[c, m] = w * jnp.exp(-r * (float(tokens - steps + 1) - segf * float(steps)))

    next(forward)

    @pl.loop(0, groups)
    def _(c):
        lam = [lam_t[c, m] for m in range(MODES)]
        w = [w_t[c, m] for m in range(MODES)]

        def block(jb, state):
            for inner in range(4):
                j = jb * 4 + inner
                value = u[c, token_rows(j), :]
                state = [lam[m] * state[m] + value for m in range(MODES)]
                y[c, token_rows(j), :] = add_up([w[m] * state[m] for m in range(MODES)])
            return state

        lax.fori_loop(0, steps // 4, block, [ex_t[c, m] for m in range(MODES)])

    next(forward)
    for load in loads[3:]:
        load.wait()
    spread(qb, qf)
    spread(cb, sf, gain_v)
    sq[...] = jnp.zeros_like(sq)
    cs[...] = jnp.zeros_like(cs)
    next(forward)
    next(forward)

    @pl.loop(0, groups)
    def _(c):
        lam = [lam_t[c, m] for m in range(MODES)]
        start = [cf_t[c, m] * wide(incoming[0, c, pl.ds(m, 1), :]) for m in range(MODES)]

        def block(jb, state):
            for inner in range(4):
                j = jb * 4 + inner
                at_j = token_rows(j)
                conv = y[c, at_j, :] + add_up(state)
                state = [lam[m] * state[m] for m in range(MODES)]
                y[c, at_j, :] = conv
                mixed = qf[c, at_j, :] * conv
                sq[j] = sq[j] + mixed * mixed
                cs[j] = cs[j] + sf[c, at_j, :] * mixed
            return state

        lax.fori_loop(0, steps // 4, block, start)

    packed = jnp.zeros((SUB, LANES), F32)

    def pack(jb, packed):
        for inner in range(4):
            j = jb * 4 + inner
            packed = jnp.where(lane == j, jnp.sum(sq[j], axis=1, keepdims=True), packed)
            packed = jnp.where(lane == j + steps, jnp.sum(cs[j], axis=1, keepdims=True), packed)
        return packed

    packed = lax.fori_loop(0, steps // 4, pack, packed)
    msg[...] = packed
    posts = [
        pltpu.make_async_remote_copy(
            src_ref=msg,
            dst_ref=tp_buf.at[i - 1],
            send_sem=tp_send.at[i - 1],
            recv_sem=tp_recv.at[i - 1],
            device_id=(place, mates[i - 1]),
            device_id_type=MESH,
        )
        for i in range(1, ntp)
    ]
    for post in posts:
        post.start()
    for post in posts:
        post.wait_recv()
    sends.extend(posts)
    sums = add_up([packed] + [tp_buf[i] for i in range(ntp - 1)]) * (1.0 / total_width)
    inv = 1.0 / jnp.sqrt(sums + 1e-06)
    proj = pltpu.roll(sums, LANES - steps, 1) * (inv * inv * inv)
    for j in range(steps):
        inv_t[j] = jnp.broadcast_to(inv[:, j : j + 1], (SUB, LANES))
        proj_t[j] = jnp.broadcast_to(proj[:, j : j + 1], (SUB, LANES))

    @pl.loop(0, groups)
    def _(c):
        lam = [lam_t[c, m] for m in range(MODES)]

        def block(jb, state):
            for inner in range(4):
                j = steps - 1 - (jb * 4 + inner)
                at_j = token_rows(j)
                q = qf[c, at_j, :]
                mixed = q * y[c, at_j, :]
                value = (inv_t[j] * sf[c, at_j, :] - mixed * proj_t[j]) * q
                cg[c, at_j, :] = value
                state = [lam[m] * state[m] + value for m in range(MODES)]
            return state

        state = lax.fori_loop(0, steps // 4, block, [jnp.zeros((SUB, LANES), F32)] * MODES)
        gather_segments(c, state, True)

    backward = exchange(1)
    next(backward)

    @pl.loop(0, groups)
    def _(c):
        lam = [lam_t[c, m] for m in range(MODES)]
        w = [w_t[c, m] for m in range(MODES)]

        def block(jb, state):
            for inner in range(4):
                j = steps - 1 - (jb * 4 + inner)
                at_j = token_rows(j)
                value = cg[c, at_j, :]
                state = [lam[m] * state[m] + value for m in range(MODES)]
                u[c, at_j, :] = add_up([w[m] * state[m] for m in range(MODES)])
            return state

        lax.fori_loop(0, steps // 4, block, [ex_t[c, m] for m in range(MODES)])

    next(backward)

    @pl.loop(0, groups)
    def _(c):
        scale = wide(gain_v[pl.ds(c, 1), :])

        def block(jb, carry):
            for inner in range(4):
                j = jb * 4 + inner
                at_j = token_rows(j)
                conv = y[c, at_j, :]
                mixed = qf[c, at_j, :] * conv
                inv_j = inv_t[j]
                nm[c, at_j, :] = mixed * inv_j * scale
                qg[c, at_j, :] = (inv_j * sf[c, at_j, :] - mixed * proj_t[j]) * conv
            return carry

        lax.fori_loop(0, steps // 4, block, 0)

    next(backward)

    def round_out(src, dst):
        @pl.loop(0, groups)
        def _(c):
            for t in range(0, tokens, 32):
                dst[t : t + 32, cols(c)] = src[c, t : t + 32, :].astype(dst.dtype)

    round_out(nm, gb)
    store_normed = pltpu.make_async_copy(gb, normed, out_sem.at[0])
    store_normed.start()
    round_out(qg, cb)
    store_query = pltpu.make_async_copy(cb, query_grad, out_sem.at[1])
    store_query.start()
    next(backward)
    next(backward)

    @pl.loop(0, groups)
    def _(c):
        lam = [lam_t[c, m] for m in range(MODES)]
        start = [cb_t[c, m] * wide(incoming[1, c, pl.ds(m, 1), :]) for m in range(MODES)]

        def block(jb, state):
            for inner in range(4):
                j = steps - 1 - (jb * 4 + inner)
                at_j = token_rows(j)
                u[c, at_j, :] = u[c, at_j, :] + add_up(state)
                state = [lam[m] * state[m] for m in range(MODES)]
            return state

        lax.fori_loop(0, steps // 4, block, start)

    round_out(u, qb)
    store_gated = pltpu.make_async_copy(qb, gated_grad, out_sem.at[2])
    store_gated.start()
    for one in sends:
        one.wait_send()
    store_normed.wait()
    store_query.wait()
    store_gated.wait()


def shape_of(ctx):
    return (8, 4) if ctx == 128 else (2, ctx // (2 * NJ))


def solution(mesh):
    ntp, ctx = mesh.shape["tp"], mesh.shape["ctx"]
    ny, nk = shape_of(ctx)

    def per_device(query, gated, cotangent, rate, residue, gain):
        tokens, width = query.shape
        groups = width // LANES
        part = groups // NJ
        steps = tokens // SUB
        vmem = lambda *shape: pltpu.VMEM(shape, F32)
        half = pltpu.VMEM((tokens, width), jnp.bfloat16)
        copies = 2 * (NJ - 1) + (nk - 1) + (ny - 1)
        anywhere = pl.BlockSpec(memory_space=pl.ANY)
        return pl.pallas_call(
            functools.partial(kernel, ny, nk, ntp),
            out_shape=[jax.ShapeDtypeStruct((tokens, width), jnp.bfloat16)] * 3,
            in_specs=[anywhere] * 6,
            out_specs=[anywhere] * 3,
            scratch_shapes=[half] * 3
            + [vmem(MODES, width), vmem(MODES, width), vmem(groups, LANES)]
            + [vmem(groups, tokens, LANES)] * 7
            + [vmem(groups, MODES, LANES)]
            + [vmem(groups, MODES, SUB, LANES)] * 5
            + [
                vmem(2, groups, MODES, LANES),
                vmem(2, groups, MODES, LANES),
                vmem(2, NJ - 1, part, MODES, LANES),
                vmem(2, max(nk - 1, 1), part, MODES, LANES),
                vmem(2, max(ny - 1, 1), part, MODES, LANES),
                vmem(2, part, MODES, LANES),
                vmem(2, part, MODES, LANES),
                vmem(2, NJ - 1, part, MODES, LANES),
            ]
            + [vmem(steps, SUB, LANES)] * 2
            + [vmem(SUB, LANES), vmem(max(ntp - 1, 1), SUB, LANES)]
            + [vmem(steps, SUB, LANES)] * 2
            + [
                pltpu.SemaphoreType.DMA((6,)),
                pltpu.SemaphoreType.DMA((3,)),
                pltpu.SemaphoreType.DMA((2, copies)),
                pltpu.SemaphoreType.DMA((2, copies)),
                pltpu.SemaphoreType.DMA((max(ntp - 1, 1),)),
                pltpu.SemaphoreType.DMA((max(ntp - 1, 1),)),
            ],
            compiler_params=pltpu.CompilerParams(collective_id=0, has_side_effects=True),
            name="hyena",
        )(query, gated, cotangent, rate.T, residue.T, gain.reshape(groups, LANES))

    return jax.shard_map(
        per_device,
        mesh=mesh,
        in_specs=(P("ctx", "tp"), P("ctx", "tp"), P("ctx", "tp"), P("tp", None), P("tp", None), P("tp")),
        out_specs=(P("ctx", "tp"),) * 3,
        check_vma=False,
    )
```

time: 1190 us -> 80.7 us (0.07)
  the two profiles are of different devices: /device:TPU:6 before, /device:TPU:8 now
where the time goes in v1:
time: 80.7 us; the launch traced here: 80.5 us
  Pallas kernels  75.9 us (94%)
  local copies, waits for them, and re-layouts  3.95 us (5%)
    pallas_call x1, Pallas kernels, per_device(): pl.pallas_call(functools.partial(kernel, ny, nk, ntp), out_shape=[jax.Sha...  75.9 us
    unnamed x7, local copies, waits for them, and re-layouts  3.95 us

profile of v1, /device:TPU:8, one launch (start us, length us, event | category | flops | bytes accessed | tf_op | source)
XLA Modules:
  0.0 80.5 jit_solution(6322382178823988751)
XLA Ops:
  0.6 75.9 %hyena.1 = (bf16[256,1024]{1,0:T(8,128)(2,1)}, bf16[256,1024]{1,0:T(8,128)(2,1)}, bf16[256,1024]{1,0:T(8,128)(2,1)}) custom-call(bf16[256,1024]{1,0:T(8,128)(2,1)} %query.1, bf16[256,1024]{1,0:T(8,128)(2,1)} %gated.1, bf16[256,1024]{1,0:T(8,128)(2,1)} %cotangent.1, f32[8,1024]{1,0:T(8,128)} %bitcast.3, f32[8,1024]{1,0:T(8,128)} %bitcast.4, f32[8,128]{1,0:T(8,128)} %bitcast.5), custom_call_target="tpu_custom_call" | custom-call | tf_op jit(solution)/shard_map/hyena/pallas_call | solution.py:444
  76.5 0.0 copy-start.1
  76.5 1.9 %copy.12 = bf16[256,1024]{1,0:T(8,128)(2,1)} copy(bf16[256,1024]{1,0:T(8,128)(2,1)} %get-tuple-element.6) | data formatting | bytes 1048576
  78.4 0.0 copy-done.1
  78.4 0.0 copy-start
  78.4 0.8 copy.13
  79.2 0.4 copy-done
  79.7 0.8 copy.14
Async XLA Ops:
  76.5 1.9 %copy-start.1 = (bf16[256,1024]{1,0:T(8,128)(2,1)S(1)}, bf16[256,1024]{1,0:T(8,128)(2,1)}, u32[]{:S(2)}) copy-start(bf16[256,1024]{1,0:T(8,128)(2,1)} %get-tuple-element.7) | copy-start | bytes 1572868
  78.4 1.2 %copy-start = (bf16[256,1024]{1,0:T(8,128)(2,1)S(1)}, bf16[256,1024]{1,0:T(8,128)(2,1)}, u32[]{:S(2)}) copy-start(bf16[256,1024]{1,0:T(8,128)(2,1)} %get-tuple-element.8) | copy-start | bytes 1572868

commit v2 on v1

v2 whole, which is shorter than its diff:
```python
import functools

import jax
import jax.numpy as jnp
from jax import lax
from jax.experimental import pallas as pl
from jax.experimental.pallas import tpu as pltpu
from jax.sharding import PartitionSpec as P

MESH = pl.DeviceIdType.MESH
MODES = 8
SUB = 8
LANES = 128
PAD = 4
PARTS = 4
STEP = 8
F32 = jnp.float32


def add_up(terms):
    while len(terms) > 1:
        terms = [a + b for a, b in zip(terms[::2], terms[1::2])] + ([terms[-1]] if len(terms) % 2 else [])
    return terms[0]


def kernel(
    ny, nz, ntp,
    query, gated, cotangent, rate, residue, gain,
    normed, query_grad, u, behind, lam_t, cb_t,
    qb, gb, cb, rate_v, residue_v, gain_v,
    y, qf, sf, cg, nm, qg,
    rt, w_t, cf_t, ex_t,
    states, incoming, z_buf, y_buf, t_out, in_out, p_buf,
    sq, cs, msg, tp_buf, inv_t, proj_t,
    in_sem, send_sem, recv_sem, tp_send, tp_recv,
):
    tokens, width = qb.shape
    groups = width // LANES
    steps = tokens // SUB
    seq_total = tokens * nz * ny
    total_width = width * ntp
    place = lax.axis_index("ctx")
    column = lax.axis_index("tp")
    yy = place // nz
    zz = lax.rem(place, nz)

    def at(y_, z_):
        return y_ * nz + z_

    z_targets = [lax.rem(zz + i, nz) for i in range(1, nz)]
    y_targets = [lax.rem(yy + i, ny) for i in range(1, ny)]
    mates = [lax.rem(column + i, ntp) for i in range(1, ntp)]

    barrier = pltpu.get_barrier_semaphore()
    for other in [at(yy, z) for z in z_targets] + [at(y_, zz) for y_ in y_targets]:
        pl.semaphore_signal(barrier, inc=1, device_id=(other, column), device_id_type=MESH)
    for mate in mates:
        pl.semaphore_signal(barrier, inc=1, device_id=(place, mate), device_id_type=MESH)

    loads = [
        pltpu.make_async_copy(src, dst, in_sem.at[n])
        for n, (src, dst) in enumerate(
            [(rate, rate_v), (residue, residue_v), (gated, gb), (query, qb), (cotangent, cb), (gain, gain_v)]
        )
    ]
    for load in loads:
        load.start()

    seg = lax.broadcasted_iota(jnp.int32, (SUB, LANES), 0)
    segf = seg.astype(F32)
    lane = lax.broadcasted_iota(jnp.int32, (SUB, LANES), 1)

    def cols(c):
        return pl.ds(pl.multiple_of(c * LANES, LANES), LANES)

    def wide(row):
        return jnp.broadcast_to(row, (SUB, LANES))

    def token_rows(j):
        return pl.ds(j, SUB, stride=steps + PAD)

    def spread(src, dst, scale=None):
        @pl.loop(0, groups)
        def _(c):
            for n in range(SUB):
                tile = src[n * steps : (n + 1) * steps, cols(c)].astype(F32)
                dst[c, pl.ds(n * (steps + PAD), steps), :] = tile if scale is None else tile * scale[pl.ds(c, 1), :]

    def gather_segments(c, state, reverse):
        for m in range(MODES):
            r = wide(rate_v[pl.ds(m, 1), cols(c)])
            x = state[m]
            for hop in (1, 2, 4):
                decay = jnp.exp(-r * float(steps * hop))
                if reverse:
                    x = x + jnp.where(seg < SUB - hop, decay, 0.0) * pltpu.roll(x, SUB - hop, 0)
                else:
                    x = x + jnp.where(seg >= hop, decay, 0.0) * pltpu.roll(x, hop, 0)
            if reverse:
                states[1, c, pl.ds(m, 1), :] = x[0:1]
                ex_t[c, m] = jnp.where(seg < SUB - 1, pltpu.roll(x, SUB - 1, 0), 0.0)
            else:
                states[0, c, pl.ds(m, 1), :] = x[SUB - 1 : SUB]
                ex_t[c, m] = jnp.where(seg >= 1, pltpu.roll(x, 1, 0), 0.0)

    def decays(c):
        lam = [lam_t[c, m] for m in range(MODES)]
        lam4 = [a * a for a in lam]
        return lam, [a * a for a in lam4]

    def accumulate(lam, lam4, state, values):
        for n in range(0, len(values), 4):
            fresh = [
                (lam[m] * values[n] + values[n + 1]) * (lam[m] * lam[m]) + (lam[m] * values[n + 2] + values[n + 3])
                for m in range(MODES)
            ]
            state = [lam4[m] * state[m] + fresh[m] for m in range(MODES)]
        return state

    loads[0].wait()
    loads[1].wait()

    @pl.loop(0, groups)
    def _(c):
        rates = rate_v[:, cols(c)]
        rt[c] = rates
        residue_v[:, cols(c)] = residue_v[:, cols(c)] * jnp.sqrt(2.0 * rates + 1.0 / seq_total)
        for m in range(MODES):
            lam_t[c, m] = jnp.exp(-wide(rate_v[pl.ds(m, 1), cols(c)]))

    loads[2].wait()
    spread(gb, u)

    @pl.loop(0, groups)
    def _(c):
        lam, lam4 = decays(c)

        def block(jb, state):
            values = [u[c, token_rows(jb * STEP + n), :] for n in range(STEP)]
            return accumulate(lam, lam4, state, values)

        state = lax.fori_loop(0, steps // STEP, block, [jnp.zeros((SUB, LANES), F32)] * MODES)
        gather_segments(c, state, False)

    pl.semaphore_wait(barrier, len(z_targets) + len(y_targets) + len(mates))

    sends = []

    def copy(src, dst, way, number, device):
        out = pltpu.make_async_remote_copy(
            src_ref=src,
            dst_ref=dst,
            send_sem=send_sem.at[way, number],
            recv_sem=recv_sem.at[way, number],
            device_id=device,
            device_id_type=MESH,
        )
        sends.append(out)
        return out

    def exchange(way):
        turn = (lambda items: items[::-1]) if way else (lambda items: items)
        mirror = lambda p, n: (n - 1 - p) if way else p
        piece = lax.rem(zz, groups)
        block_decay = jnp.exp(-rt[piece] * float(tokens))
        row_decay = jnp.exp(-rt[piece] * float(tokens * nz))

        first = [
            copy(states.at[way, lax.rem(target, groups)], z_buf.at[way, zz], way, i, (at(yy, target), column))
            for i, target in enumerate(z_targets)
        ]
        for one in first:
            one.start()
        z_buf[way, zz] = states[way, piece]
        yield
        for one in first:
            one.wait_recv()
        total = jnp.zeros((MODES, LANES), F32)
        enter = {}
        for z in turn(list(range(nz))):
            enter[z] = total
            total = block_decay * total + z_buf[way, z]
        t_out[way] = total
        base = nz - 1
        second = [
            copy(t_out.at[way], y_buf.at[way, yy], way, base + i, (at(target, zz), column))
            for i, target in enumerate(y_targets)
        ]
        for one in second:
            one.start()
        yield
        for z in range(nz):
            p_buf[z] = enter[z]
        y_buf[way, yy] = total
        reached = [lax.rem(zz + nz - groups // 2 + i, nz) for i in range(groups)]
        decays_to = [jnp.exp(-rt[piece] * (mirror(z, nz) * tokens).astype(F32)) for z in reached]
        entering = [p_buf[z] for z in reached]
        for one in second:
            one.wait_recv()
        above = jnp.zeros((MODES, LANES), F32)
        for y_ in turn(list(range(ny))):
            is_before = (y_ > yy) if way else (y_ < yy)
            above = jnp.where(is_before, row_decay * above + y_buf[way, y_], above)
        base = base + ny - 1
        third = []
        for i, z in enumerate(reached):
            result = entering[i] + decays_to[i] * above
            if i == groups // 2:
                own = result
            else:
                number = len(third)
                in_out[way, number] = result
                one = copy(in_out.at[way, number], incoming.at[way, piece], way, base + number, (at(yy, z), column))
                one.start()
                third.append(one)
        incoming[way, piece] = own
        yield
        for one in third:
            one.wait_recv()
        yield

    forward = exchange(0)
    next(forward)

    @pl.loop(0, groups)
    def _(c):
        for m in range(MODES):
            w = wide(residue_v[pl.ds(m, 1), cols(c)])
            r = wide(rate_v[pl.ds(m, 1), cols(c)])
            w_t[c, m] = w
            cf_t[c, m] = w * jnp.exp(-r * (segf * float(steps) + 1.0))
            cb_t[c, m] = w * jnp.exp(-r * (float(tokens - steps + 1) - segf * float(steps)))

    @pl.loop(0, groups)
    def _(c):
        lam = [lam_t[c, m] for m in range(MODES)]
        w = [w_t[c, m] for m in range(MODES)]

        def block(jb, state):
            values = [u[c, token_rows(jb * STEP + n), :] for n in range(STEP)]
            results = []
            for value in values:
                state = [lam[m] * state[m] + value for m in range(MODES)]
                results.append(add_up([w[m] * state[m] for m in range(MODES)]))
            for n in range(STEP):
                y[c, token_rows(jb * STEP + n), :] = results[n]
            return state

        lax.fori_loop(0, steps // STEP, block, [ex_t[c, m] for m in range(MODES)])

    for load in loads[3:]:
        load.wait()
    spread(qb, qf)
    spread(cb, sf, gain_v)
    sq[...] = jnp.zeros_like(sq)
    cs[...] = jnp.zeros_like(cs)
    next(forward)
    next(forward)
    next(forward)

    @pl.loop(0, groups)
    def _(c):
        lam = [lam_t[c, m] for m in range(MODES)]
        start = [cf_t[c, m] * wide(incoming[0, c, pl.ds(m, 1), :]) for m in range(MODES)]

        def block(jb, state):
            here = [jb * STEP + n for n in range(STEP)]
            old = [y[c, token_rows(j), :] for j in here]
            qs = [qf[c, token_rows(j), :] for j in here]
            ss = [sf[c, token_rows(j), :] for j in here]
            sq_old = [sq[j] for j in here]
            cs_old = [cs[j] for j in here]
            conv = []
            for n in range(STEP):
                conv.append(old[n] + add_up(state))
                state = [lam[m] * state[m] for m in range(MODES)]
            mixed = [a * b for a, b in zip(qs, conv)]
            sq_new = [a + b * b for a, b in zip(sq_old, mixed)]
            cs_new = [a + b * d for a, b, d in zip(cs_old, mixed, ss)]
            for n, j in enumerate(here):
                y[c, token_rows(j), :] = conv[n]
                sq[j] = sq_new[n]
                cs[j] = cs_new[n]
            return state

        lax.fori_loop(0, steps // STEP, block, start)

    packed = jnp.zeros((SUB, LANES), F32)

    def pack(jb, packed):
        for inner in range(4):
            j = jb * 4 + inner
            packed = jnp.where(lane == j, jnp.sum(sq[j], axis=1, keepdims=True), packed)
            packed = jnp.where(lane == j + steps, jnp.sum(cs[j], axis=1, keepdims=True), packed)
        return packed

    packed = lax.fori_loop(0, steps // 4, pack, packed)
    msg[...] = packed
    posts = [
        pltpu.make_async_remote_copy(
            src_ref=msg,
            dst_ref=tp_buf.at[i - 1],
            send_sem=tp_send.at[i - 1],
            recv_sem=tp_recv.at[i - 1],
            device_id=(place, mates[i - 1]),
            device_id_type=MESH,
        )
        for i in range(1, ntp)
    ]
    for post in posts:
        post.start()
    for post in posts:
        post.wait_recv()
    sends.extend(posts)
    sums = add_up([packed] + [tp_buf[i] for i in range(ntp - 1)]) * (1.0 / total_width)
    inv = 1.0 / jnp.sqrt(sums + 1e-06)
    proj = pltpu.roll(sums, LANES - steps, 1) * (inv * inv * inv)
    for j in range(steps):
        inv_t[j] = jnp.broadcast_to(inv[:, j : j + 1], (SUB, LANES))
        proj_t[j] = jnp.broadcast_to(proj[:, j : j + 1], (SUB, LANES))

    @pl.loop(0, groups)
    def _(c):
        lam, lam4 = decays(c)

        def block(jb, state):
            here = [steps - 1 - (jb * STEP + n) for n in range(STEP)]
            qs = [qf[c, token_rows(j), :] for j in here]
            convs = [y[c, token_rows(j), :] for j in here]
            ss = [sf[c, token_rows(j), :] for j in here]
            invs = [inv_t[j] for j in here]
            projs = [proj_t[j] for j in here]
            values = [
                (i * s - q * v * p) * q for q, v, s, i, p in zip(qs, convs, ss, invs, projs)
            ]
            state = accumulate(lam, lam4, state, values)
            for n, j in enumerate(here):
                cg[c, token_rows(j), :] = values[n]
            return state

        state = lax.fori_loop(0, steps // STEP, block, [jnp.zeros((SUB, LANES), F32)] * MODES)
        gather_segments(c, state, True)

    backward = exchange(1)
    next(backward)

    @pl.loop(0, groups)
    def _(c):
        lam = [lam_t[c, m] for m in range(MODES)]
        w = [w_t[c, m] for m in range(MODES)]

        def block(jb, state):
            here = [steps - 1 - (jb * STEP + n) for n in range(STEP)]
            values = [cg[c, token_rows(j), :] for j in here]
            results = []
            for value in values:
                state = [lam[m] * state[m] + value for m in range(MODES)]
                results.append(add_up([w[m] * state[m] for m in range(MODES)]))
            for n, j in enumerate(here):
                u[c, token_rows(j), :] = results[n]
            return state

        lax.fori_loop(0, steps // STEP, block, [ex_t[c, m] for m in range(MODES)])

    @pl.loop(0, groups)
    def _(c):
        scale = wide(gain_v[pl.ds(c, 1), :])

        def block(jb, carry):
            here = [jb * STEP + n for n in range(STEP)]
            convs = [y[c, token_rows(j), :] for j in here]
            mixed = [qf[c, token_rows(j), :] * v for j, v in zip(here, convs)]
            invs = [inv_t[j] for j in here]
            grads = [
                (i * sf[c, token_rows(j), :] - x * proj_t[j]) * v for j, i, x, v in zip(here, invs, mixed, convs)
            ]
            for n, j in enumerate(here):
                nm[c, token_rows(j), :] = mixed[n] * invs[n] * scale
                qg[c, token_rows(j), :] = grads[n]
            return carry

        lax.fori_loop(0, steps // STEP, block, 0)

    def round_out(src, dst):
        @pl.loop(0, groups)
        def _(c):
            for n in range(SUB):
                dst[n * steps : (n + 1) * steps, cols(c)] = src[c, pl.ds(n * (steps + PAD), steps), :].astype(dst.dtype)

    round_out(nm, normed)
    round_out(qg, query_grad)
    next(backward)
    next(backward)
    next(backward)
    behind[...] = incoming[1]
    for one in sends:
        one.wait_send()


def finish(normed_v, query_v, u, behind, lam_t, cb_t, normed, query_grad, gated_grad, out, full, sem):
    groups = u.shape[0]
    tokens = out.shape[0]
    steps = tokens // SUB
    early = [
        pltpu.make_async_copy(normed_v, normed, sem.at[0]),
        pltpu.make_async_copy(query_v, query_grad, sem.at[1]),
    ]
    for one in early:
        one.start()
    late = []
    share = groups // PARTS
    for number in range(PARTS):

        @pl.loop(number * share, (number + 1) * share)
        def _(c):
            lam = [lam_t[c, m] for m in range(MODES)]
            start = [
                cb_t[c, m] * jnp.broadcast_to(behind[c, pl.ds(m, 1), :], (SUB, LANES)) for m in range(MODES)
            ]

            def block(jb, state):
                here = [pl.ds(steps - 1 - (jb * STEP + n), SUB, stride=steps + PAD) for n in range(STEP)]
                results = []
                for old in [u[c, rows, :] for rows in here]:
                    results.append(old + add_up(state))
                    state = [lam[m] * state[m] for m in range(MODES)]
                for n, rows in enumerate(here):
                    full[c, rows, :] = results[n]
                return state

            lax.fori_loop(0, steps // STEP, block, start)
            cols = pl.ds(pl.multiple_of(c * LANES, LANES), LANES)
            for n in range(SUB):
                out[n * steps : (n + 1) * steps, cols] = full[c, pl.ds(n * (steps + PAD), steps), :].astype(out.dtype)

        span = pl.ds(number * share * LANES, share * LANES)
        one = pltpu.make_async_copy(out.at[:, span], gated_grad.at[:, span], sem.at[2 + number])
        one.start()
        late.append(one)
    for one in early + late:
        one.wait()


def shape_of(ctx):
    return ctx // 16, 16


def solution(mesh):
    ntp, ctx = mesh.shape["tp"], mesh.shape["ctx"]
    ny, nz = shape_of(ctx)

    def per_device(query, gated, cotangent, rate, residue, gain):
        tokens, width = query.shape
        groups = width // LANES
        steps = tokens // SUB
        vmem = lambda *shape: pltpu.VMEM(shape, F32)
        half = pltpu.VMEM((tokens, width), jnp.bfloat16)
        copies = (nz - 1) + (ny - 1) + (groups - 1)
        anywhere = pl.BlockSpec(memory_space=pl.ANY)
        in_vmem = pl.BlockSpec(memory_space=pltpu.VMEM)
        states = vmem(groups, MODES, SUB, LANES)
        values = vmem(groups, tokens + SUB * PAD, LANES)
        held = pl.pallas_call(
            functools.partial(kernel, ny, nz, ntp),
            out_shape=[half, half, values, vmem(groups, MODES, LANES), states, states],
            in_specs=[anywhere] * 6,
            out_specs=[in_vmem] * 6,
            scratch_shapes=[half] * 3
            + [vmem(MODES, width), vmem(MODES, width), vmem(groups, LANES)]
            + [values] * 6
            + [vmem(groups, MODES, LANES)]
            + [states] * 3
            + [
                vmem(2, groups, MODES, LANES),
                vmem(2, groups, MODES, LANES),
                vmem(2, nz, MODES, LANES),
                vmem(2, ny, MODES, LANES),
                vmem(2, MODES, LANES),
                vmem(2, groups - 1, MODES, LANES),
                vmem(nz, MODES, LANES),
            ]
            + [vmem(steps, SUB, LANES)] * 2
            + [vmem(SUB, LANES), vmem(max(ntp - 1, 1), SUB, LANES)]
            + [vmem(steps, SUB, LANES)] * 2
            + [
                pltpu.SemaphoreType.DMA((6,)),
                pltpu.SemaphoreType.DMA((2, copies)),
                pltpu.SemaphoreType.DMA((2, copies)),
                pltpu.SemaphoreType.DMA((max(ntp - 1, 1),)),
                pltpu.SemaphoreType.DMA((max(ntp - 1, 1),)),
            ],
            compiler_params=pltpu.CompilerParams(collective_id=0, has_side_effects=True),
            name="hyena",
        )(query, gated, cotangent, rate.T, residue.T, gain.reshape(groups, LANES))
        return pl.pallas_call(
            finish,
            out_shape=[jax.ShapeDtypeStruct((tokens, width), jnp.bfloat16)] * 3,
            in_specs=[in_vmem] * 6,
            out_specs=[anywhere] * 3,
            scratch_shapes=[half, values, pltpu.SemaphoreType.DMA((2 + PARTS,))],
            name="finish",
        )(*[pltpu.with_memory_space_constraint(one, pltpu.VMEM) for one in held])

    return jax.shard_map(
        per_device,
        mesh=mesh,
        in_specs=(P("ctx", "tp"), P("ctx", "tp"), P("ctx", "tp"), P("tp", None), P("tp", None), P("tp")),
        out_specs=(P("ctx", "tp"),) * 3,
        check_vma=False,
    )
```

time: 80.7 us -> 67.2 us (0.83)
  the two profiles are of different devices: /device:TPU:8 before, /device:TPU:16 now
where the time goes in v2:
time: 67.2 us; the launch traced here: 67.1 us
  Pallas kernels  66.4 us (99%)
    pallas_call x1, Pallas kernels, per_device(): pl.pallas_call(functools.partial(kernel, ny, nz, ntp), out_shape=[half, h...  64.8 us
    pallas_call x1, Pallas kernels, per_device(): pl.pallas_call(finish, out_shape=[jax.ShapeDtypeStruct((tokens, width), j...  1.6 us

profile of v2, /device:TPU:16, one launch (start us, length us, event | category | flops | bytes accessed | tf_op | source)
XLA Modules:
  0.0 67.1 jit_solution(6601734977396174602)
XLA Ops:
  0.6 64.8 %hyena.1 = (bf16[256,1024]{1,0:T(8,128)(2,1)S(1)}, bf16[256,1024]{1,0:T(8,128)(2,1)S(1)}, f32[8,288,128]{2,1,0:T(8,128)S(1)}, f32[8,8,128]{2,1,0:T(8,128)S(1)}, ...) custom-call(bf16[256,1024]{1,0:T(8,128)(2,1)} %query.1, bf16[256,1024]{1,0:T(8,128)(2,1)} %gated.1, ...), custom_call_target="tpu_custom_call" | custom-call | tf_op jit(solution)/shard_map/hyena/pallas_call | solution.py:463
  65.5 1.6 %finish.1 = (bf16[256,1024]{1,0:T(8,128)(2,1)}, bf16[256,1024]{1,0:T(8,128)(2,1)}, bf16[256,1024]{1,0:T(8,128)(2,1)}) custom-call(bf16[256,1024]{1,0:T(8,128)(2,1)S(1)} %get-tuple-element.9.normed_v, bf16[256,1024]{1,0:T(8,128)(2,1)S(1)} %get-tuple-element.10.query_v, f32[8,288,128]{2,1,0:T(8,128)S(1)} %get-tuple-element.11.u, ...), custom_call_target="tpu_custom_call" | custom-call | tf_op jit(solution)/shard_map/finish/pallas_call | solution.py:495

commit v3 on v2

--- a/solution.py
+++ b/solution.py
@@ -12,7 +12,8 @@
 SUB = 8
 LANES = 128
 PAD = 4
-PARTS = 4
+ORDER = (0, 1, 7, 2, 6, 3, 5, 4)
+NEAREST = (0, 1, -1, 2, -2, 3, -3, -4)
 STEP = 8
 F32 = jnp.float32
 
@@ -26,10 +27,10 @@
 def kernel(
     ny, nz, ntp,
     query, gated, cotangent, rate, residue, gain,
-    normed, query_grad, u, behind, lam_t, cb_t,
+    normed, query_grad, gated_grad,
     qb, gb, cb, rate_v, residue_v, gain_v,
-    y, qf, sf, cg, nm, qg,
-    rt, w_t, cf_t, ex_t,
+    u, y, qf, sf, cg, nm, qg,
+    rt, lam_t, w_t, cf_t, cb_t, ex_t,
     states, incoming, z_buf, y_buf, t_out, in_out, p_buf,
     sq, cs, msg, tp_buf, inv_t, proj_t,
     in_sem, send_sem, recv_sem, tp_send, tp_recv,
@@ -131,19 +132,6 @@
     loads[2].wait()
     spread(gb, u)
 
-    @pl.loop(0, groups)
-    def _(c):
-        lam, lam4 = decays(c)
-
-        def block(jb, state):
-            values = [u[c, token_rows(jb * STEP + n), :] for n in range(STEP)]
-            return accumulate(lam, lam4, state, values)
-
-        state = lax.fori_loop(0, steps // STEP, block, [jnp.zeros((SUB, LANES), F32)] * MODES)
-        gather_segments(c, state, False)
-
-    pl.semaphore_wait(barrier, len(z_targets) + len(y_targets) + len(mates))
-
     sends = []
 
     def copy(src, dst, way, number, device):
@@ -162,17 +150,20 @@
         turn = (lambda items: items[::-1]) if way else (lambda items: items)
         mirror = lambda p, n: (n - 1 - p) if way else p
         piece = lax.rem(zz, groups)
+        first = []
         block_decay = jnp.exp(-rt[piece] * float(tokens))
         row_decay = jnp.exp(-rt[piece] * float(tokens * nz))
 
-        first = [
-            copy(states.at[way, lax.rem(target, groups)], z_buf.at[way, zz], way, i, (at(yy, target), column))
-            for i, target in enumerate(z_targets)
-        ]
-        for one in first:
-            one.start()
+        for shift in ORDER:
+            c = lax.rem(zz + shift, groups)
+            for i in (shift, shift + groups):
+                if i == 0:
+                    continue
+                one = copy(states.at[way, c], z_buf.at[way, zz], way, i - 1, (at(yy, z_targets[i - 1]), column))
+                one.start()
+                first.append(one)
+            yield
         z_buf[way, zz] = states[way, piece]
-        yield
         for one in first:
             one.wait_recv()
         total = jnp.zeros((MODES, LANES), F32)
@@ -192,7 +183,7 @@
         for z in range(nz):
             p_buf[z] = enter[z]
         y_buf[way, yy] = total
-        reached = [lax.rem(zz + nz - groups // 2 + i, nz) for i in range(groups)]
+        reached = [lax.rem(zz + nz + e, nz) for e in NEAREST]
         decays_to = [jnp.exp(-rt[piece] * (mirror(z, nz) * tokens).astype(F32)) for z in reached]
         entering = [p_buf[z] for z in reached]
         for one in second:
@@ -202,25 +193,46 @@
             is_before = (y_ > yy) if way else (y_ < yy)
             above = jnp.where(is_before, row_decay * above + y_buf[way, y_], above)
         base = base + ny - 1
-        third = []
-        for i, z in enumerate(reached):
+        third = [None] * groups
+        for i in reversed(range(groups)):
             result = entering[i] + decays_to[i] * above
-            if i == groups // 2:
-                own = result
+            if i == 0:
+                incoming[way, piece] = result
             else:
-                number = len(third)
-                in_out[way, number] = result
-                one = copy(in_out.at[way, number], incoming.at[way, piece], way, base + number, (at(yy, z), column))
-                one.start()
-                third.append(one)
-        incoming[way, piece] = own
+                in_out[way, i - 1] = result
+                third[i] = copy(
+                    in_out.at[way, i - 1], incoming.at[way, piece], way, base + i - 1, (at(yy, reached[i]), column)
+                )
+                third[i].start()
+        for i in range(groups):
+            yield
+            if i:
+                third[i].wait_recv()
         yield
-        for one in third:
-            one.wait_recv()
-        yield
+
+    def arriving(i):
+        return lax.rem(zz + 2 * groups - NEAREST[i], groups)
+
+    def forward_states(c):
+        lam, lam4 = decays(c)
+
+        def block(jb, state):
+            values = [u[c, token_rows(jb * STEP + n), :] for n in range(STEP)]
+            return accumulate(lam, lam4, state, values)
+
+        state = lax.fori_loop(0, steps // STEP, block, [jnp.zeros((SUB, LANES), F32)] * MODES)
+        gather_segments(c, state, False)
 
     forward = exchange(0)
-    next(forward)
+    early = groups // 2
+    for shift in ORDER[:early]:
+        forward_states(lax.rem(zz + shift, groups))
+    pl.semaphore_wait(barrier, len(z_targets) + len(y_targets) + len(mates))
+    for _ in range(early):
+        next(forward)
+    for shift in ORDER[early:]:
+        forward_states(lax.rem(zz + shift, groups))
+        next(forward)
 
     @pl.loop(0, groups)
     def _(c):
@@ -230,6 +242,14 @@
             w_t[c, m] = w
             cf_t[c, m] = w * jnp.exp(-r * (segf * float(steps) + 1.0))
             cb_t[c, m] = w * jnp.exp(-r * (float(tokens - steps + 1) - segf * float(steps)))
+
+    for load in loads[3:]:
+        load.wait()
+    spread(qb, qf)
+    spread(cb, sf, gain_v)
+    sq[...] = jnp.zeros_like(sq)
+    cs[...] = jnp.zeros_like(cs)
+    next(forward)
 
     @pl.loop(0, groups)
     def _(c):
@@ -248,18 +268,9 @@
 
         lax.fori_loop(0, steps // STEP, block, [ex_t[c, m] for m in range(MODES)])
 
-    for load in loads[3:]:
-        load.wait()
-    spread(qb, qf)
-    spread(cb, sf, gain_v)
-    sq[...] = jnp.zeros_like(sq)
-    cs[...] = jnp.zeros_like(cs)
     next(forward)
-    next(forward)
-    next(forward)
-
-    @pl.loop(0, groups)
-    def _(c):
+
+    def add_earlier(c):
         lam = [lam_t[c, m] for m in range(MODES)]
         start = [cf_t[c, m] * wide(incoming[0, c, pl.ds(m, 1), :]) for m in range(MODES)]
 
@@ -284,6 +295,10 @@
             return state
 
         lax.fori_loop(0, steps // STEP, block, start)
+
+    for i in range(groups):
+        next(forward)
+        add_earlier(arriving(i))
 
     packed = jnp.zeros((SUB, LANES), F32)
 
@@ -319,8 +334,7 @@
         inv_t[j] = jnp.broadcast_to(inv[:, j : j + 1], (SUB, LANES))
         proj_t[j] = jnp.broadcast_to(proj[:, j : j + 1], (SUB, LANES))
 
-    @pl.loop(0, groups)
-    def _(c):
+    def gradient_states(c):
         lam, lam4 = decays(c)
 
         def block(jb, state):
@@ -342,7 +356,9 @@
         gather_segments(c, state, True)
 
     backward = exchange(1)
-    next(backward)
+    for shift in ORDER:
+        gradient_states(lax.rem(zz + shift, groups))
+        next(backward)
 
     @pl.loop(0, groups)
     def _(c):
@@ -391,54 +407,41 @@
     round_out(qg, query_grad)
     next(backward)
     next(backward)
-    next(backward)
-    behind[...] = incoming[1]
+
+    def add_later(c):
+        lam = [lam_t[c, m] for m in range(MODES)]
+        start = [cb_t[c, m] * wide(incoming[1, c, pl.ds(m, 1), :]) for m in range(MODES)]
+
+        def block(jb, state):
+            here = [steps - 1 - (jb * STEP + n) for n in range(STEP)]
+            results = []
+            for old in [u[c, token_rows(j), :] for j in here]:
+                results.append(old + add_up(state))
+                state = [lam[m] * state[m] for m in range(MODES)]
+            for n, j in enumerate(here):
+                u[c, token_rows(j), :] = results[n]
+            return state
+
+        lax.fori_loop(0, steps // STEP, block, start)
+        for n in range(SUB):
+            gated_grad[n * steps : (n + 1) * steps, cols(c)] = u[c, pl.ds(n * (steps + PAD), steps), :].astype(
+                gated_grad.dtype
+            )
+
+    for i in range(groups):
+        next(backward)
+        add_later(arriving(i))
     for one in sends:
         one.wait_send()
 
 
-def finish(normed_v, query_v, u, behind, lam_t, cb_t, normed, query_grad, gated_grad, out, full, sem):
-    groups = u.shape[0]
-    tokens = out.shape[0]
-    steps = tokens // SUB
-    early = [
-        pltpu.make_async_copy(normed_v, normed, sem.at[0]),
-        pltpu.make_async_copy(query_v, query_grad, sem.at[1]),
-    ]
-    for one in early:
-        one.start()
-    late = []
-    share = groups // PARTS
-    for number in range(PARTS):
-
-        @pl.loop(number * share, (number + 1) * share)
-        def _(c):
-            lam = [lam_t[c, m] for m in range(MODES)]
-            start = [
-                cb_t[c, m] * jnp.broadcast_to(behind[c, pl.ds(m, 1), :], (SUB, LANES)) for m in range(MODES)
-            ]
-
-            def block(jb, state):
-                here = [pl.ds(steps - 1 - (jb * STEP + n), SUB, stride=steps + PAD) for n in range(STEP)]
-                results = []
-                for old in [u[c, rows, :] for rows in here]:
-                    results.append(old + add_up(state))
-                    state = [lam[m] * state[m] for m in range(MODES)]
-                for n, rows in enumerate(here):
-                    full[c, rows, :] = results[n]
-                return state
-
-            lax.fori_loop(0, steps // STEP, block, start)
-            cols = pl.ds(pl.multiple_of(c * LANES, LANES), LANES)
-            for n in range(SUB):
-                out[n * steps : (n + 1) * steps, cols] = full[c, pl.ds(n * (steps + PAD), steps), :].astype(out.dtype)
-
-        span = pl.ds(number * share * LANES, share * LANES)
-        one = pltpu.make_async_copy(out.at[:, span], gated_grad.at[:, span], sem.at[2 + number])
-        one.start()
-        late.append(one)
-    for one in early + late:
-        one.wait()
+def finish(normed_v, query_v, gated_v, normed, query_grad, gated_grad, sem):
+    pairs = [(normed_v, normed), (query_v, query_grad), (gated_v, gated_grad)]
+    stores = [pltpu.make_async_copy(src, dst, sem.at[n]) for n, (src, dst) in enumerate(pairs)]
+    for store in stores:
+        store.start()
+    for store in stores:
+        store.wait()
 
 
 def shape_of(ctx):
@@ -462,14 +465,14 @@
         values = vmem(groups, tokens + SUB * PAD, LANES)
         held = pl.pallas_call(
             functools.partial(kernel, ny, nz, ntp),
-            out_shape=[half, half, values, vmem(groups, MODES, LANES), states, states],
+            out_shape=[half] * 3,
             in_specs=[anywhere] * 6,
-            out_specs=[in_vmem] * 6,
+            out_specs=[in_vmem] * 3,
             scratch_shapes=[half] * 3
             + [vmem(MODES, width), vmem(MODES, width), vmem(groups, LANES)]
-            + [values] * 6
+            + [values] * 7
             + [vmem(groups, MODES, LANES)]
-            + [states] * 3
+            + [states] * 5
             + [
                 vmem(2, groups, MODES, LANES),
                 vmem(2, groups, MODES, LANES),
@@ -495,9 +498,9 @@
         return pl.pallas_call(
             finish,
             out_shape=[jax.ShapeDtypeStruct((tokens, width), jnp.bfloat16)] * 3,
-            in_specs=[in_vmem] * 6,
+            in_specs=[in_vmem] * 3,
             out_specs=[anywhere] * 3,
-            scratch_shapes=[half, values, pltpu.SemaphoreType.DMA((2 + PARTS,))],
+            scratch_shapes=[pltpu.SemaphoreType.DMA((3,))],
             name="finish",
         )(*[pltpu.with_memory_space_constraint(one, pltpu.VMEM) for one in held])
 

time: 67.2 us -> 63.7 us (0.948)
  the two profiles are of different devices: /device:TPU:16 before, /device:TPU:8 now
where the time goes in v3:
time: 63.7 us; the launch traced here: 63.6 us
  Pallas kernels  62.9 us (99%)
  between operations  0.64 us (1%)
    pallas_call x1, Pallas kernels, per_device(): pl.pallas_call(functools.partial(kernel, ny, nz, ntp), out_shape=[half] *...  61.7 us

profile of v3, /device:TPU:8, one launch (start us, length us, event | category | flops | bytes accessed | tf_op | source)
XLA Modules:
  0.0 63.6 jit_solution(10903094277045818656)
XLA Ops:
  0.6 61.7 %hyena.1 = (bf16[256,1024]{1,0:T(8,128)(2,1)S(1)}, bf16[256,1024]{1,0:T(8,128)(2,1)S(1)}, bf16[256,1024]{1,0:T(8,128)(2,1)S(1)}) custom-call(bf16[256,1024]{1,0:T(8,128)(2,1)} %query.1, bf16[256,1024]{1,0:T(8,128)(2,1)} %gated.1, bf16[256,1024]{1,0:T(8,128)(2,1)} %cotangent.1, f32[8,1024]{1,0:T(8,128)} %bitcast.3, f32[8,1024]{1,0:T(8,128)} %bitcast.4, ...), custom_call_target="tpu_custom_call" | custom-call | tf_op jit(solution)/shard_map/hyena/pallas_call | solution.py:466
  62.4 1.2 %finish.1 = (bf16[256,1024]{1,0:T(8,128)(2,1)}, bf16[256,1024]{1,0:T(8,128)(2,1)}, bf16[256,1024]{1,0:T(8,128)(2,1)}) custom-call(bf16[256,1024]{1,0:T(8,128)(2,1)S(1)} %get-tuple-element.6.normed_v, bf16[256,1024]{1,0:T(8,128)(2,1)S(1)} %get-tuple-element.7.query_v, bf16[256,1024]{1,0:T(8,128)(2,1)S(1)} %get-tuple-element.8.gated_v), custom_call_target="tpu_custom_call" | custom-call | tf_op jit(solution)/shard_map/finish/pallas_call | solution.py:498

commit v4 on v3

--- a/solution.py
+++ b/solution.py
@@ -49,11 +49,13 @@
         return y_ * nz + z_
 
     z_targets = [lax.rem(zz + i, nz) for i in range(1, nz)]
+    z_targets_by = [(min(i + 1, nz - i - 1), i) for i in range(nz - 1)]
     y_targets = [lax.rem(yy + i, ny) for i in range(1, ny)]
     mates = [lax.rem(column + i, ntp) for i in range(1, ntp)]
 
     barrier = pltpu.get_barrier_semaphore()
-    for other in [at(yy, z) for z in z_targets] + [at(y_, zz) for y_ in y_targets]:
+    far_first = sorted(z_targets_by, reverse=True)
+    for other in [at(yy, z_targets[i]) for _, i in far_first] + [at(y_, zz) for y_ in y_targets]:
         pl.semaphore_signal(barrier, inc=1, device_id=(other, column), device_id_type=MESH)
     for mate in mates:
         pl.semaphore_signal(barrier, inc=1, device_id=(place, mate), device_id_type=MESH)
@@ -405,7 +407,14 @@
 
     round_out(nm, normed)
     round_out(qg, query_grad)
+
+    def settle():
+        while sends:
+            sends.pop().wait_send()
+
+    settle()
     next(backward)
+    settle()
     next(backward)
 
     def add_later(c):
@@ -431,8 +440,8 @@
     for i in range(groups):
         next(backward)
         add_later(arriving(i))
-    for one in sends:
-        one.wait_send()
+        if i == 0:
+            settle()
 
 
 def finish(normed_v, query_v, gated_v, normed, query_grad, gated_grad, sem):

time: 63.7 us -> 63.6 us (level)
  no operation moved by 1% of the time
where the time goes in v4:
time: 63.6 us; the launch traced here: 63.4 us
  Pallas kernels  62.8 us (99%)
  between operations  0.64 us (1%)
    pallas_call x1, Pallas kernels, per_device(): pl.pallas_call(functools.partial(kernel, ny, nz, ntp), out_shape=[half] *...  61.6 us

profile of v4, /device:TPU:8, one launch (start us, length us, event | category | flops | bytes accessed | tf_op | source)
XLA Modules:
  0.0 63.4 jit_solution(16791633742024987380)
XLA Ops:
  0.6 61.6 %hyena.1 = (bf16[256,1024]{1,0:T(8,128)(2,1)S(1)}, bf16[256,1024]{1,0:T(8,128)(2,1)S(1)}, bf16[256,1024]{1,0:T(8,128)(2,1)S(1)}) custom-call(bf16[256,1024]{1,0:T(8,128)(2,1)} %query.1, bf16[256,1024]{1,0:T(8,128)(2,1)} %gated.1, bf16[256,1024]{1,0:T(8,128)(2,1)} %cotangent.1, f32[8,1024]{1,0:T(8,128)} %bitcast.3, f32[8,1024]{1,0:T(8,128)} %bitcast.4, ...), custom_call_target="tpu_custom_call" | custom-call | tf_op jit(solution)/shard_map/hyena/pallas_call | solution.py:475
  62.3 1.2 %finish.1 = (bf16[256,1024]{1,0:T(8,128)(2,1)}, bf16[256,1024]{1,0:T(8,128)(2,1)}, bf16[256,1024]{1,0:T(8,128)(2,1)}) custom-call(bf16[256,1024]{1,0:T(8,128)(2,1)S(1)} %get-tuple-element.6.normed_v, bf16[256,1024]{1,0:T(8,128)(2,1)S(1)} %get-tuple-element.7.query_v, bf16[256,1024]{1,0:T(8,128)(2,1)S(1)} %get-tuple-element.8.gated_v), custom_call_target="tpu_custom_call" | custom-call | tf_op jit(solution)/shard_map/finish/pallas_call | solution.py:507
